TPU v7x, 256 devices: a whole 4x4x8 slice. The times are simulated.
256 devices in a mesh: tm: 8 (over z_hi, y), space: 32 (over z_lo, x, core).
Axes of the slice: x: 4, y: 4, z: 8 (z_hi: 2, z_lo: 4; z = z_hi * 4 + z_lo), core: 2. Of those that a mesh axis runs over, the one named last changes fastest.
Arguments:
- member_average: float32 [128, 2880, 640], P('tm', 'space'), may hold values from -6 to 6
- member_spread_squared: float32 [128, 2880, 640], P('tm', 'space'), may hold values from 0.1 to 4
- measured_truth: float32 [128, 2880, 640], P('tm', 'space'), may hold values from -8 to 8
- coefficients: float32 [4, 2880, 640], P(None, 'space'), may hold values from -1 to 1
Outputs:
- updated: float32 [4, 2880, 640], P(None, 'space')
All inputs are finite; a program needn't handle non-finite values.
Results may differ from a plain program's by a relative error of at most 0.00002.
Values sent between devices are 32-bit elements; how exact they have to be, the bound alone decides.
No kernel may reach another device: no remote copies, remote signals or barrier semaphores. Data moves between devices by JAX's collectives and lax.ppermute only.
A program may use at most 64 MiB of HBM per device.

v0:
```python
import jax
import jax.numpy as jnp
from jax import lax
from jax.sharding import PartitionSpec as P

ITERS = 2
descent_factor = 0.5
smooth_weight = 0.03


def padded(block, sides, width):
    for axis, dim in sides:
        count = lax.axis_size(axis)
        forward = [(i, i + 1) for i in range(count - 1)]
        forward.append((count - 1, 0))
        backward = [(target, source) for source, target in forward]
        low = lax.ppermute(
            lax.slice_in_dim(block, block.shape[dim] - width, None, axis=dim), axis, forward
        )
        high = lax.ppermute(lax.slice_in_dim(block, 0, width, axis=dim), axis, backward)
        block = jnp.concatenate([low, block, high], axis=dim)
    return block


def laplace_rim(extended):
    middle = extended[:, 1:-1, :]
    along_lon = extended[:, 2:, :] + extended[:, :-2, :] - 2.0 * middle
    steps_lat = middle[..., 1:] - middle[..., :-1]
    zero_col = jnp.zeros(middle.shape[:-1] + (1,), jnp.float32)
    along_lat = jnp.concatenate([steps_lat, zero_col], axis=-1) - jnp.concatenate(
        [zero_col, steps_lat], axis=-1
    )
    return along_lon + along_lat


def daily_score_parts(calibration_coefficients_set, fmean, fvar, obs):
    base_exp = jnp.exp(calibration_coefficients_set[2])
    spread = jnp.sqrt(
        base_exp + calibration_coefficients_set[3] * calibration_coefficients_set[3] * fvar
    )
    center = calibration_coefficients_set[0] + calibration_coefficients_set[1] * fmean
    standard = (obs - center) / spread
    cumulative = 0.5 * (1.0 + jax.scipy.special.erf(standard * 0.7071067811865476))
    density = jnp.exp(-0.5 * standard * standard) * 0.3989422804014327
    dcenter = 1.0 - 2.0 * cumulative
    dvar = (2.0 * density - 0.5641895835477563) / (2.0 * spread)
    return jnp.stack(
        [
            jnp.sum(dcenter, axis=0),
            jnp.sum(dcenter * fmean, axis=0),
            jnp.sum(dvar * base_exp, axis=0),
            jnp.sum(dvar * 2.0 * calibration_coefficients_set[3] * fvar, axis=0),
        ]
    )


def smoothing(calibration_coefficients_set):
    first = laplace_rim(padded(calibration_coefficients_set, (("space", 1),), 1))
    return laplace_rim(padded(first, (("space", 1),), 1))


def apply_update(calibration_coefficients_set, partial_sum, roughness_cost, every_day_total):
    aggregate_loss = lax.psum(partial_sum, "tm")
    return calibration_coefficients_set - descent_factor * (
        aggregate_loss / every_day_total + roughness_cost
    )


def on_device(member_average, member_spread_squared, measured_truth, coefficients):
    calibration_coefficients_set = coefficients
    every_day_total = member_average.shape[0] * lax.axis_size("tm")
    for step in range(ITERS):
        partial_sum = daily_score_parts(
            calibration_coefficients_set, member_average, member_spread_squared, measured_truth
        )
        roughness_cost = smooth_weight * smoothing(calibration_coefficients_set)
        calibration_coefficients_set = apply_update(
            calibration_coefficients_set, partial_sum, roughness_cost, every_day_total
        )
    return calibration_coefficients_set


def solution(mesh):
    placed = (
        P("tm", "space", None),
        P("tm", "space", None),
        P("tm", "space", None),
        P(None, "space", None),
    )
    return jax.shard_map(
        on_device, mesh=mesh, in_specs=placed, out_specs=P(None, "space", None), check_vma=False
    )
```

profile of v0, /device:TPU:2, one launch (start us, length us, event | category | flops | bytes accessed | tf_op | source)
XLA Modules:
  0.0 270.6 jit_solution(1380413186751168871)
XLA Ops:
  6.5 1.4 copy.16
  8.0 0.8 copy-done
  8.9 5.4 %add_subtract_fusion.1 = (f32[16,90,640]{2,0,1:T(8,128)S(1)}, f32[16,90,640]{2,0,1:T(8,128)S(1)}) fusion(f32[16,90,640]{2,0,1:T(8,128)} %param.5, f32[90,640]{1,0:T(8,128)S(1)} %get-tuple-element.27, f32[90,640]{1,0:T(8,128)S(1)} %get-tuple-element.28, f32[16,90,640]{2,0,1:T(8,128)} %param.6, f32[16,90,640]{2,0,1:T(8,128)S(1)} %copy-done, ...), kind=kLoop, calls=%fused_computation.19 | loop fusion | flops 8294400 | bytes 19353600 | tf_op jit(solution)/shard_map/sub | solution.py:45
  14.3 1.7 fusion.31
  15.9 0.4 copy-done.2
  16.3 4.6 %multiply_reduce_fusion.4 = (f32[90,640]{1,0:T(8,128)S(1)}, f32[90,640]{1,0:T(8,128)S(1)}) fusion(f32[90,640]{1,0:T(8,128)S(1)} %get-tuple-element.28, f32[16,90,640]{2,0,1:T(8,128)S(1)} %copy-done.2, f32[90,640]{1,0:T(8,128)S(1)} %get-tuple-element.27, f32[16,90,640]{2,0,1:T(8,128)S(1)} %get-tuple-element.16, f32[90,640]{1,0:T(8,128)S(1)} %get-tuple-element.26), kind=kLoop, calls=%fused_computation.17 | loop fusion | flops 11865600 | bytes 8524800 | tf_op jit(solution)/shard_map/reduce_sum | solution.py:51
  20.9 1.0 pad_maximum_fusion.8
  22.0 0.7 fusion.35
  22.9 0.6 collective-permute-start.1
  23.8 0.5 collective-permute-done
  24.2 2.4 collective-permute-done.1
  26.7 0.4 fusion.27
  27.1 3.9 %collective-permute-start.2 = (f32[4,1,640]{2,1,0:T(1,128)S(1)}, f32[4,1,640]{2,1,0:T(1,128)S(1)}, u32[]{:S(2)}, u32[]{:S(2)}) collective-permute-start(f32[4,1,640]{2,1,0:T(1,128)S(1)} %get-tuple-element.31), channel_id=1, source_target_pairs={{1,0},{2,1},{3,2},{4,3},{5,4},{6,5},{7,6},{8,7},{9,8},{10,9},{11,1... | collective-permute-start | bytes 30728 | tf_op jit(solution)/shard_map/ppermute | solution.py:20
  31.4 1.1 collective-permute-done.2
  32.4 6.3 %collective-permute-done.3 = f32[4,1,640]{2,1,0:T(1,128)S(1)} collective-permute-done((f32[4,1,640]{2,1,0:T(1,128)S(1)}, f32[4,1,640]{2,1,0:T(1,128)S(1)}, u32[]{:S(2)}, u32[]{:S(2)}) %collective-permute-start.3) | collective-permute-done | bytes 10272 | tf_op jit(solution)/shard_map/ppermute | solution.py:17
  38.7 98.3 %all-reduce.11.cloned.1.call-done = f32[4,90,640]{2,1,0:T(8,128)} async-done(((f32[4,90,640]{2,1,0:T(8,128)}), f32[4,90,640]{2,1,0:T(8,128)}) %all-reduce.11.cloned.1.call-update) | async-done | bytes 921616 | tf_op jit(solution)/shard_map/psum | solution.py:63
  137.1 2.2 fusion.24
  139.7 5.4 %add_subtract_fusion = (f32[16,90,640]{2,0,1:T(8,128)S(1)}, f32[16,90,640]{2,0,1:T(8,128)S(1)}) fusion(f32[16,90,640]{2,0,1:T(8,128)} %param.5, f32[90,640]{1,0:T(8,128)S(1)} %get-tuple-element.18, f32[90,640]{1,0:T(8,128)S(1)} %get-tuple-element.19, f32[16,90,640]{2,0,1:T(8,128)} %param.6, f32[16,90,640]{2,0,1:T(8,128)S(1)} %copy-done.1, ...), kind=kLoop, calls=%fused_computation.13 | loop fusion | flops 8294400 | bytes 19353600 | tf_op jit(solution)/shard_map/sub | solution.py:45
  145.1 1.7 fusion.30
  146.8 0.4 copy-done.3
  147.2 4.6 %multiply_reduce_fusion.1 = (f32[90,640]{1,0:T(8,128)S(1)}, f32[90,640]{1,0:T(8,128)S(1)}) fusion(f32[90,640]{1,0:T(8,128)S(1)} %get-tuple-element.19, f32[16,90,640]{2,0,1:T(8,128)S(1)} %copy-done.3, f32[90,640]{1,0:T(8,128)S(1)} %get-tuple-element.18, f32[16,90,640]{2,0,1:T(8,128)S(1)} %get-tuple-element.14, f32[90,640]{1,0:T(8,128)S(1)} %get-tuple-element.17), kind=kLoop, calls=%fused_computation.11 | loop fusion | flops 11865600 | bytes 8524800 | tf_op jit(solution)/shard_map/reduce_sum | solution.py:51
  151.8 1.0 pad_maximum_fusion.9
  152.9 0.5 collective-permute-start.5
  153.8 0.6 collective-permute-done.4
  154.3 1.8 collective-permute-done.5
  156.1 0.4 fusion.17
  156.6 0.5 collective-permute-start.7
  157.5 0.6 collective-permute-done.6
  158.0 4.5 %collective-permute-done.7 = f32[4,1,640]{2,1,0:T(1,128)S(1)} collective-permute-done((f32[4,1,640]{2,1,0:T(1,128)S(1)}, f32[4,1,640]{2,1,0:T(1,128)S(1)}, u32[]{:S(2)}, u32[]{:S(2)}) %collective-permute-start.7) | collective-permute-done | bytes 10272 | tf_op jit(solution)/shard_map/ppermute | solution.py:17
  162.6 97.9 %all-reduce.13.cloned.1.call-done = f32[4,90,640]{2,1,0:T(8,128)} async-done(((f32[4,90,640]{2,1,0:T(8,128)}), f32[4,90,640]{2,1,0:T(8,128)}) %all-reduce.13.cloned.1.call-update) | async-done | bytes 921616 | tf_op jit(solution)/shard_map/psum | solution.py:63
  260.4 1.8 fusion.14
  262.2 1.5 copy.17
  (24 shorter events, 2.2 us)
Async XLA Ops:
  6.5 130.6 %all-reduce.11.cloned.1.call-start = ((), (), s32[]{:S(2)}) async-start(), calls=%async_computation | async-start | bytes 1966080 | tf_op jit(solution)/shard_map/psum | solution.py:63
  6.5 2.3 copy-start
  14.3 2.0 copy-start.2
  22.0 238.5 %all-reduce.13.cloned.1.call-start = ((), (), s32[]{:S(2)}) async-start(), calls=%async_computation.1 | async-start | bytes 1966080 | tf_op jit(solution)/shard_map/psum | solution.py:63
  22.8 1.5 collective-permute-start
  22.9 3.8 %collective-permute-start.1 = (f32[4,1,640]{2,1,0:T(1,128)S(1)}, f32[4,1,640]{2,1,0:T(1,128)S(1)}, u32[]{:S(2)}, u32[]{:S(2)}) collective-permute-start(f32[4,1,640]{2,1,0:T(1,128)S(1)} %copy.11), channel_id=1, source_target_pairs={{0,1},{1,2},{2,3},{3,4},{4,5},{5,6},{6,7},{7,8},{8,9},{9,10},{10,1... | collective-permute-start | bytes 30728 | tf_op jit(solution)/shard_map/ppermute | solution.py:17
  27.1 5.3 %collective-permute-start.2 = (f32[4,1,640]{2,1,0:T(1,128)S(1)}, f32[4,1,640]{2,1,0:T(1,128)S(1)}, u32[]{:S(2)}, u32[]{:S(2)}) collective-permute-start(f32[4,1,640]{2,1,0:T(1,128)S(1)} %get-tuple-element.31), channel_id=1, source_target_pairs={{1,0},{2,1},{3,2},{4,3},{5,4},{6,5},{7,6},{8,7},{9,8},{10,9},{11,1... | collective-permute-start | bytes 30728 | tf_op jit(solution)/shard_map/ppermute | solution.py:20
  31.1 7.7 %collective-permute-start.3 = (f32[4,1,640]{2,1,0:T(1,128)S(1)}, f32[4,1,640]{2,1,0:T(1,128)S(1)}, u32[]{:S(2)}, u32[]{:S(2)}) collective-permute-start(f32[4,1,640]{2,1,0:T(1,128)S(1)} %get-tuple-element.32), channel_id=1, source_target_pairs={{0,1},{1,2},{2,3},{3,4},{4,5},{5,6},{6,7},{7,8},{8,9},{9,10},{10,1... | collective-permute-start | bytes 30728 | tf_op jit(solution)/shard_map/ppermute | solution.py:17
  137.1 2.6 copy-start.1
  145.1 2.0 copy-start.3
  152.8 1.5 collective-permute-start.4
  152.9 3.2 %collective-permute-start.5 = (f32[4,1,640]{2,1,0:T(1,128)S(1)}, f32[4,1,640]{2,1,0:T(1,128)S(1)}, u32[]{:S(2)}, u32[]{:S(2)}) collective-permute-start(f32[4,1,640]{2,1,0:T(1,128)S(1)} %get-tuple-element.25), channel_id=1, source_target_pairs={{0,1},{1,2},{2,3},{3,4},{4,5},{5,6},{6,7},{7,8},{8,9},{9,10},{10,1... | collective-permute-start | bytes 30728 | tf_op jit(solution)/shard_map/ppermute | solution.py:17
  156.6 1.5 collective-permute-start.6
  156.6 5.9 %collective-permute-start.7 = (f32[4,1,640]{2,1,0:T(1,128)S(1)}, f32[4,1,640]{2,1,0:T(1,128)S(1)}, u32[]{:S(2)}, u32[]{:S(2)}) collective-permute-start(f32[4,1,640]{2,1,0:T(1,128)S(1)} %get-tuple-element.23), channel_id=1, source_target_pairs={{0,1},{1,2},{2,3},{3,4},{4,5},{5,6},{6,7},{7,8},{8,9},{9,10},{10,1... | collective-permute-start | bytes 30728 | tf_op jit(solution)/shard_map/ppermute | solution.py:17
Sparse Core Ops, SparseCore 0:
  22.1 114.9 all-reduce.10
  153.0 107.4 all-reduce.12
where the time goes:
time: 271 us
  waiting for transfers between devices  214 us (79%)
  other arithmetic  31.7 us (12%)
  between operations  13.6 us (5%)
  starting transfers between devices  5.8 us (2%)
  local copies, waits for them, and re-layouts  5.58 us (2%)
    psum x2, waiting for transfers between devices, apply_update(): aggregate_loss = lax.psum(partial_sum, 'tm')  196 us
    ppermute x4, waiting for transfers between devices, padded(): lax.ppermute(lax.slice_in_dim(block, block.shape[dim] - width, None, axis...  15.1 us
    sub x2, other arithmetic, daily_score_parts(): dcenter = 1.0 - 2.0 * cumulative  10.8 us
    reduce_sum x2, other arithmetic, daily_score_parts(): jnp.sum(dvar * base_exp, axis=0)  9.22 us
  transfers between devices with their start and end apart: 10, of which 10 were waited for; matrix products, arithmetic and copies ran while one was open for 1% of the time, Pallas kernels for 0%

commit v1 on v0

--- a/solution.py
+++ b/solution.py
@@ -60,7 +60,8 @@
 
 
 def apply_update(calibration_coefficients_set, partial_sum, roughness_cost, every_day_total):
-    aggregate_loss = lax.psum(partial_sum, "tm")
+    terms = lax.all_gather(partial_sum, "tm", axis=0, tiled=False)
+    aggregate_loss = terms.sum(axis=0)
     return calibration_coefficients_set - descent_factor * (
         aggregate_loss / every_day_total + roughness_cost
     )

time: 271 us -> 385 us (1.42)
  waiting for transfers between devices: 214 us -> 318 us
  other arithmetic: 31.7 us -> 41.4 us
    all_gather x0 -> x2, waiting for transfers between devices: none -> 313 us  [apply_update(): terms = lax.all_gather(partial_sum, 'tm', axis=0, tiled=False)]
    psum x2 -> x0, waiting for transfers between devices: 196 us -> none  [apply_update(): aggregate_loss = lax.psum(partial_sum, 'tm')]
    ppermute x4, waiting for transfers between devices: 15.1 us -> 4.22 us  [padded(): lax.ppermute(lax.slice_in_dim(block, block.shape[dim] - width, None, axis...]
    reduce_sum x0 -> x2, other arithmetic: none -> 9.58 us  [apply_update(): aggregate_loss = terms.sum(axis=0)]
  transfers between devices with their start and end apart: 10 -> 10, of which waited for: 10 -> 6; matrix products, arithmetic and copies ran while one was open for 1% -> 3% of each run, Pallas kernels for 0% -> 0%
where the time goes in v1:
time: 385 us
  waiting for transfers between devices  318 us (83%)
  other arithmetic  41.4 us (11%)
  between operations  13.6 us (4%)
  starting transfers between devices  5.8 us (2%)
  local copies, waits for them, and re-layouts  5.6 us (1%)
    all_gather x2, waiting for transfers between devices, apply_update(): terms = lax.all_gather(partial_sum, 'tm', axis=0, tiled=False)  313 us
    sub x2, other arithmetic, daily_score_parts(): dcenter = 1.0 - 2.0 * cumulative  10.8 us
    reduce_sum x2, other arithmetic, apply_update(): aggregate_loss = terms.sum(axis=0)  9.58 us
    reduce_sum x2, other arithmetic, daily_score_parts(): jnp.sum(dvar * base_exp, axis=0)  9.22 us
  transfers between devices with their start and end apart: 10, of which 6 were waited for; matrix products, arithmetic and copies ran while one was open for 3% of the time, Pallas kernels for 0%

profile of v1, /device:TPU:2, one launch (start us, length us, event | category | flops | bytes accessed | tf_op | source)
XLA Modules:
  0.0 384.8 jit_solution(7305542938247314441)
XLA Ops:
  6.5 1.4 copy.29
  8.0 0.8 copy-done
  8.9 5.4 %add_subtract_fusion.1 = (f32[16,90,640]{2,0,1:T(8,128)S(1)}, f32[16,90,640]{2,0,1:T(8,128)S(1)}) fusion(f32[16,90,640]{2,0,1:T(8,128)} %param.5, f32[90,640]{1,0:T(8,128)S(1)} %get-tuple-element.27, f32[90,640]{1,0:T(8,128)S(1)} %get-tuple-element.28, f32[16,90,640]{2,0,1:T(8,128)} %param.6, f32[16,90,640]{2,0,1:T(8,128)S(1)} %copy-done, ...), kind=kLoop, calls=%fused_computation.19 | loop fusion | flops 8294400 | bytes 19353600 | tf_op jit(solution)/shard_map/sub | solution.py:45
  14.3 1.7 fusion.31
  15.9 0.4 copy-done.2
  16.3 4.6 %multiply_reduce_fusion.4 = (f32[90,640]{1,0:T(8,128)S(1)}, f32[90,640]{1,0:T(8,128)S(1)}) fusion(f32[90,640]{1,0:T(8,128)S(1)} %get-tuple-element.28, f32[16,90,640]{2,0,1:T(8,128)S(1)} %copy-done.2, f32[90,640]{1,0:T(8,128)S(1)} %get-tuple-element.27, f32[16,90,640]{2,0,1:T(8,128)S(1)} %get-tuple-element.16, f32[90,640]{1,0:T(8,128)S(1)} %get-tuple-element.26), kind=kLoop, calls=%fused_computation.17 | loop fusion | flops 11865600 | bytes 8524800 | tf_op jit(solution)/shard_map/reduce_sum | solution.py:51
  20.9 1.1 pad_maximum_fusion.8
  22.1 0.7 fusion.35
  23.0 0.6 collective-permute-start.1
  23.9 0.5 collective-permute-done
  24.3 2.4 collective-permute-done.1
  26.8 0.4 fusion.27
  27.2 3.9 %collective-permute-start.2 = (f32[4,1,640]{2,1,0:T(1,128)S(1)}, f32[4,1,640]{2,1,0:T(1,128)S(1)}, u32[]{:S(2)}, u32[]{:S(2)}) collective-permute-start(f32[4,1,640]{2,1,0:T(1,128)S(1)} %get-tuple-element.31), channel_id=1, source_target_pairs={{1,0},{2,1},{3,2},{4,3},{5,4},{6,5},{7,6},{8,7},{9,8},{10,9},{11,1... | collective-permute-start | bytes 30728 | tf_op jit(solution)/shard_map/ppermute | solution.py:20
  31.2 0.3 slice_subtract_fusion.2
  31.5 158.4 %all-gather.5.cloned.1.call-done = f32[32,90,640]{2,1,0:T(8,128)} async-done(((f32[4,90,640]{2,1,0:T(8,128)}), f32[32,90,640]{2,1,0:T(8,128)}) %all-gather.5.cloned.1.call-update) | async-done | bytes 7372816 | tf_op jit(solution)/shard_map/all_gather | solution.py:63
  189.8 4.8 %reduce_sum.94 = f32[4,90,640]{2,1,0:T(8,128)} reduce(f32[8,4,90,640]{3,2,1,0:T(8,128)} %bitcast.30, f32[]{:T(128)} %constant.12.clone.1), dimensions={0}, to_apply=%region_4.0 | reduce | flops 1612800 | bytes 8294404 | tf_op jit(solution)/shard_map/reduce_sum | solution.py:64
  194.6 2.2 fusion.24
  196.9 0.3 copy-done.1
  197.2 5.4 %add_subtract_fusion = (f32[16,90,640]{2,0,1:T(8,128)S(1)}, f32[16,90,640]{2,0,1:T(8,128)S(1)}) fusion(f32[16,90,640]{2,0,1:T(8,128)} %param.5, f32[90,640]{1,0:T(8,128)S(1)} %get-tuple-element.18, f32[90,640]{1,0:T(8,128)S(1)} %get-tuple-element.19, f32[16,90,640]{2,0,1:T(8,128)} %param.6, f32[16,90,640]{2,0,1:T(8,128)S(1)} %copy-done.1, ...), kind=kLoop, calls=%fused_computation.13 | loop fusion | flops 8294400 | bytes 19353600 | tf_op jit(solution)/shard_map/sub | solution.py:45
  202.6 1.7 fusion.30
  204.3 0.4 copy-done.3
  204.7 4.6 %multiply_reduce_fusion.1 = (f32[90,640]{1,0:T(8,128)S(1)}, f32[90,640]{1,0:T(8,128)S(1)}) fusion(f32[90,640]{1,0:T(8,128)S(1)} %get-tuple-element.19, f32[16,90,640]{2,0,1:T(8,128)S(1)} %copy-done.3, f32[90,640]{1,0:T(8,128)S(1)} %get-tuple-element.18, f32[16,90,640]{2,0,1:T(8,128)S(1)} %get-tuple-element.14, f32[90,640]{1,0:T(8,128)S(1)} %get-tuple-element.17), kind=kLoop, calls=%fused_computation.11 | loop fusion | flops 11865600 | bytes 8524800 | tf_op jit(solution)/shard_map/reduce_sum | solution.py:51
  209.3 1.1 pad_maximum_fusion.9
  210.6 0.5 collective-permute-start.5
  211.4 0.6 collective-permute-done.4
  212.0 1.8 collective-permute-done.5
  213.8 0.4 fusion.17
  214.3 0.5 collective-permute-start.7
  215.1 154.7 %all-gather.7.cloned.1.call-done = f32[32,90,640]{2,1,0:T(8,128)} async-done(((f32[4,90,640]{2,1,0:T(8,128)}), f32[32,90,640]{2,1,0:T(8,128)}) %all-gather.7.cloned.1.call-update) | async-done | bytes 7372816 | tf_op jit(solution)/shard_map/all_gather | solution.py:63
  369.8 4.8 %reduce_sum.99 = f32[4,90,640]{2,1,0:T(8,128)} reduce(f32[8,4,90,640]{3,2,1,0:T(8,128)} %bitcast.31, f32[]{:T(128)} %constant.12.clone.1), dimensions={0}, to_apply=%region_9.0 | reduce | flops 1612800 | bytes 8294404 | tf_op jit(solution)/shard_map/reduce_sum | solution.py:64
  374.6 1.8 fusion.14
  376.4 1.5 copy.30
  (26 shorter events, 1.5 us)
Async XLA Ops:
  6.5 183.3 %all-gather.5.cloned.1.call-start = ((), (), s32[]{:S(2)}) async-start(), calls=%async_computation | async-start | bytes 8847360 | tf_op jit(solution)/shard_map/all_gather | solution.py:63
  6.5 2.3 copy-start
  14.3 2.0 copy-start.2
  22.1 347.8 %all-gather.7.cloned.1.call-start = ((), (), s32[]{:S(2)}) async-start(), calls=%async_computation.1 | async-start | bytes 8847360 | tf_op jit(solution)/shard_map/all_gather | solution.py:63
  22.9 1.5 collective-permute-start
  23.0 3.8 collective-permute-start.1
  27.2 167.4 %collective-permute-start.2 = (f32[4,1,640]{2,1,0:T(1,128)S(1)}, f32[4,1,640]{2,1,0:T(1,128)S(1)}, u32[]{:S(2)}, u32[]{:S(2)}) collective-permute-start(f32[4,1,640]{2,1,0:T(1,128)S(1)} %get-tuple-element.31), channel_id=1, source_target_pairs={{1,0},{2,1},{3,2},{4,3},{5,4},{6,5},{7,6},{8,7},{9,8},{10,9},{11,1... | collective-permute-start | bytes 30728 | tf_op jit(solution)/shard_map/ppermute | solution.py:20
  31.1 163.5 %collective-permute-start.3 = (f32[4,1,640]{2,1,0:T(1,128)S(1)}, f32[4,1,640]{2,1,0:T(1,128)S(1)}, u32[]{:S(2)}, u32[]{:S(2)}) collective-permute-start(f32[4,1,640]{2,1,0:T(1,128)S(1)} %get-tuple-element.32), channel_id=1, source_target_pairs={{0,1},{1,2},{2,3},{3,4},{4,5},{5,6},{6,7},{7,8},{8,9},{9,10},{10,1... | collective-permute-start | bytes 30728 | tf_op jit(solution)/shard_map/ppermute | solution.py:17
  194.6 2.6 copy-start.1
  202.6 2.0 copy-start.3
  210.5 1.5 collective-permute-start.4
  210.6 3.2 collective-permute-start.5
  214.2 160.4 %collective-permute-start.6 = (f32[4,1,640]{2,1,0:T(1,128)S(1)}, f32[4,1,640]{2,1,0:T(1,128)S(1)}, u32[]{:S(2)}, u32[]{:S(2)}) collective-permute-start(f32[4,1,640]{2,1,0:T(1,128)S(1)} %get-tuple-element.22), channel_id=1, source_target_pairs={{1,0},{2,1},{3,2},{4,3},{5,4},{6,5},{7,6},{8,7},{9,8},{10,9},{11,1... | collective-permute-start | bytes 30728 | tf_op jit(solution)/shard_map/ppermute | solution.py:20
  214.3 160.3 %collective-permute-start.7 = (f32[4,1,640]{2,1,0:T(1,128)S(1)}, f32[4,1,640]{2,1,0:T(1,128)S(1)}, u32[]{:S(2)}, u32[]{:S(2)}) collective-permute-start(f32[4,1,640]{2,1,0:T(1,128)S(1)} %get-tuple-element.23), channel_id=1, source_target_pairs={{0,1},{1,2},{2,3},{3,4},{4,5},{5,6},{6,7},{7,8},{8,9},{9,10},{10,1... | collective-permute-start | bytes 30728 | tf_op jit(solution)/shard_map/ppermute | solution.py:17
Sparse Core Ops, SparseCore 0:
  22.2 167.5 all-gather.4
  210.6 159.2 all-gather.6
